TPU v7x, 32 devices: a whole 2x2x4 slice. The times are simulated.
32 devices in a mesh: fsdp: 16 (over z, y, core), tp: 2 (over x).
Axes of the slice: x: 2, y: 2, z: 4, core: 2. Of those that a mesh axis runs over, the one named last changes fastest.
Arguments:
- tokens: bfloat16 [16, 512, 768], P('fsdp', 'tp'), may hold values from -6 to 6
- segments: int32 [16, 512], P('fsdp'), may hold values from 0 to 2, as said below
- valid: int32 [16, 512], P('fsdp', 'tp'), may hold values from 0 to 1, as said below
- teacher: bfloat16 [16, 512, 768], P('fsdp', 'tp'), may hold values from -6 to 6
- attn_in: bfloat16 [2, 768, 3, 768], P(None, 'fsdp', None, 'tp'), may hold values from -0.3125 to 0.3125
- attn_out: bfloat16 [2, 768, 768], P(None, 'fsdp', 'tp'), may hold values from -0.625 to 0.625
- ff_in: bfloat16 [2, 768, 3072], P(None, 'fsdp', 'tp'), may hold values from -0.21875 to 0.21875
- ff_out: bfloat16 [2, 768, 3072], P(None, 'fsdp', 'tp'), may hold values from -0.109375 to 0.109375
- biases: bfloat16 [2, 5, 768], P(None, None, 'fsdp'), may hold values from -1.5 to 1.5
- gains: bfloat16 [2, 2, 768], P(None, None, 'fsdp'), may hold values from 0.5 to 1.5
- ff_bias: bfloat16 [2, 3072], P(None, 'fsdp'), may hold values from -1.5 to 1.5
- query_bias: bfloat16 [2, 768], P(None, 'fsdp'), may hold values from -1.5 to 1.5
Outputs:
- mixed: bfloat16 [16, 512, 768], P('fsdp', 'tp')
- tokens_grad: float32 [16, 512, 768], P('fsdp', 'tp')
- loss: float32 [], replicated
- attn_in_grad: float32 [2, 768, 3, 768], P(None, 'fsdp', None, 'tp')
- attn_out_grad: float32 [2, 768, 768], P(None, 'fsdp', 'tp')
- ff_in_grad: float32 [2, 768, 3072], P(None, 'fsdp', 'tp')
- ff_out_grad: float32 [2, 768, 3072], P(None, 'fsdp', 'tp')
- biases_grad: float32 [2, 5, 768], P(None, None, 'fsdp')
- gains_grad: float32 [2, 2, 768], P(None, None, 'fsdp')
- ff_bias_grad: float32 [2, 3072], P(None, 'fsdp')
- query_bias_grad: float32 [2, 768], P(None, 'fsdp')
Inputs may be any that keep to these rules, and one draw needn't show every extreme that they name: `segments`: along each sequence the ids are 1, 2, 3, ... in runs of 200 to 480 tokens (documents), then 0 (padding) to the end; padding is shorter than 480 tokens; some document of the batch has exactly 480 tokens, and some sequence consists of documents of exactly 200 tokens. `valid`: each flag is 1 independently, with a probability that rises linearly from 1/4 in the first sequence to 3/4 in the last.
All inputs are finite; a program needn't handle non-finite values.
Results may differ from a plain program's by a relative error of at most 0.035.
Values may be sent and summed in bfloat16 or wider, within the bound.
A program may use at most 192 MiB of HBM per device.

v0:
```python
import jax
import jax.numpy as jnp
from jax import lax
from jax.sharding import PartitionSpec as P

HEAD_DIM = 64


epsilon = 1e-05
root_half = 0.7071067811865476
inv_root_tau = 0.3989422804014327


def layer_norm(stream, gain, shift):
    centred = stream - jnp.mean(stream, axis=-1, keepdims=True)
    inverse = lax.rsqrt(jnp.mean(centred * centred, axis=-1, keepdims=True) + epsilon)
    normed = centred * inverse
    return (normed * gain + shift, normed, inverse)


def norm_back(grad_out, normed, inverse, gain):
    scaled = grad_out * gain
    return inverse * (
        scaled
        - jnp.mean(scaled, axis=-1, keepdims=True)
        - normed * jnp.mean(scaled * normed, axis=-1, keepdims=True)
    )


def gelu_exact(inputs):
    return 0.5 * inputs * (1.0 + lax.erf(inputs * root_half))


def gelu_slope(inputs):
    return (
        0.5 * (1.0 + lax.erf(inputs * root_half))
        + inputs * jnp.exp(-0.5 * inputs * inputs) * inv_root_tau
    )


def mask_rows(seg_ids):
    return (seg_ids[None, :] > 0) & (
        (seg_ids[:, None] == seg_ids[None, :]) | (seg_ids[:, None] == 0)
    )


def attention_forward(queries, keys_in, values_in, seg_ids):
    length = queries.shape[0]
    block_rows = min(512, length)
    score_scale = queries.shape[2] ** (-0.5)

    def one_block(block_num):
        allowed = mask_rows(seg_ids)
        scores = (
            jnp.einsum("qhd,khd->hqk", queries, keys_in, preferred_element_type=jnp.float32)
            * score_scale
        )
        scores = jnp.where(allowed[None], scores, -jnp.inf)
        highest = jnp.max(scores, axis=-1, keepdims=True)
        exponent = jnp.exp(scores - highest)
        totals = jnp.sum(exponent, axis=-1, keepdims=True)
        attn_probs = (exponent / totals).astype(jnp.bfloat16)
        mixed_rows = jnp.einsum(
            "hqk,khd->qhd", attn_probs, values_in, preferred_element_type=jnp.float32
        )
        return (mixed_rows.astype(jnp.bfloat16), (highest + jnp.log(totals))[:, :, 0])

    outputs, log_totals = lax.map(one_block, jnp.arange(length // block_rows))
    return (outputs.reshape(length, -1), log_totals)


def attention_back(queries, keys_in, values_in, seg_ids, log_totals, grad_heads):
    length = queries.shape[0]
    block_rows = min(512, length)
    score_scale = queries.shape[2] ** (-0.5)

    def one_block(sums_pair, block_item):
        block_num, log_rows = block_item
        key_sum, value_sum = sums_pair
        allowed = mask_rows(seg_ids)
        scores = (
            jnp.einsum("qhd,khd->hqk", queries, keys_in, preferred_element_type=jnp.float32)
            * score_scale
        )
        attn_probs = jnp.where(allowed[None], jnp.exp(scores - log_rows[:, :, None]), 0.0)
        value_sum = value_sum + jnp.einsum(
            "hqk,qhd->khd",
            attn_probs.astype(jnp.bfloat16),
            grad_heads,
            preferred_element_type=jnp.float32,
        )
        grad_probs = jnp.einsum(
            "qhd,khd->hqk", grad_heads, values_in, preferred_element_type=jnp.float32
        )
        grad_scores = attn_probs * (
            grad_probs - jnp.sum(attn_probs * grad_probs, axis=-1, keepdims=True)
        )
        low_scores = grad_scores.astype(jnp.bfloat16)
        query_grad = (
            jnp.einsum("hqk,khd->qhd", low_scores, keys_in, preferred_element_type=jnp.float32)
            * score_scale
        )
        key_sum = (
            key_sum
            + jnp.einsum("hqk,qhd->khd", low_scores, queries, preferred_element_type=jnp.float32)
            * score_scale
        )
        return ((key_sum, value_sum), query_grad)

    zero_sum = jnp.zeros(keys_in.shape, jnp.float32)
    (key_sum, value_sum), query_grads = lax.scan(
        one_block, (zero_sum, zero_sum), (jnp.arange(length // block_rows), log_totals)
    )
    return (query_grads.reshape(keys_in.shape), key_sum, value_sum)


def gather_rows(values_low):
    return lax.all_gather(values_low, "tp", axis=0, tiled=True)


def gather_grads(values_low):
    return lax.all_gather(values_low, "tp", axis=0, tiled=True)


def row_product(left, weight_mat):
    return lax.dot_general(
        left, weight_mat, (((1,), (1,)), ((), ())), preferred_element_type=jnp.float32
    )


def summed_rows(left, weight_mat, rows_dev):

    def term_rows(row_start, row_count):
        return row_product(left, weight_mat)

    return lax.psum_scatter(
        term_rows(jnp.int32(0), lax.axis_size("tp") * rows_dev).astype(jnp.bfloat16),
        "tp",
        scatter_dimension=0,
        tiled=True,
    ).astype(jnp.float32)


def summed_grads(left, weight_mat, rows_dev):

    def term_rows(row_start, row_count):
        return row_product(left, weight_mat)

    return lax.psum_scatter(
        term_rows(jnp.int32(0), lax.axis_size("tp") * rows_dev).astype(jnp.bfloat16),
        "tp",
        scatter_dimension=0,
        tiled=True,
    ).astype(jnp.float32)


def outer_rows(left, right):
    return lax.dot_general(
        left, right, (((0,), (0,)), ((), ())), preferred_element_type=jnp.float32
    )


def on_device(
    tokens,
    segments,
    valid,
    teacher,
    attn_in,
    attn_out,
    ff_in,
    ff_out,
    biases,
    gains,
    ff_bias,
    query_bias,
):
    rows_dev = tokens.shape[1]
    tp_rank = lax.axis_index("tp")
    tp_count = lax.axis_size("tp")
    seg_ids = segments[0]
    length = seg_ids.shape[0]
    width = tokens.shape[2]
    heads_width = attn_in.shape[3]
    hidden_width = ff_in.shape[2]
    layers = attn_in.shape[0]
    head_shape = (length, heads_width // HEAD_DIM, HEAD_DIM)
    own_seg = lax.dynamic_slice_in_dim(seg_ids, tp_rank * rows_dev, rows_dev, 0)
    weight_rows = (valid[0] * (own_seg > 0).astype(jnp.int32)).astype(jnp.float32)
    stream = tokens[0].astype(jnp.float32)
    saved_acts = []
    for layer_num in range(layers):
        fetched = (
            lax.all_gather(attn_in[layer_num], "fsdp", axis=0, tiled=True),
            lax.all_gather(attn_out[layer_num], "fsdp", axis=0, tiled=True),
            lax.all_gather(ff_in[layer_num], "fsdp", axis=0, tiled=True),
            lax.all_gather(ff_out[layer_num], "fsdp", axis=0, tiled=True),
            lax.all_gather(biases[layer_num], "fsdp", axis=1, tiled=True),
            lax.all_gather(gains[layer_num], "fsdp", axis=1, tiled=True),
            lax.all_gather(ff_bias[layer_num], "fsdp", axis=0, tiled=True),
            lax.all_gather(query_bias[layer_num], "fsdp", axis=0, tiled=True),
        )
        w_in, w_out, w_up, w_down, bias_low, gain_low, up_low, query_low = fetched
        bias_all = bias_low.astype(jnp.float32)
        gain_all = gain_low.astype(jnp.float32)
        full_in = gather_rows(stream.astype(jnp.bfloat16))
        joined_qkv = jnp.dot(
            full_in, w_in.reshape(width, 3 * heads_width), preferred_element_type=jnp.float32
        ).reshape(length, 3, heads_width)
        bias_query = lax.dynamic_slice_in_dim(
            query_low.astype(jnp.float32), tp_rank * heads_width, heads_width, 0
        )
        bias_value = lax.dynamic_slice_in_dim(bias_all[0], tp_rank * heads_width, heads_width, 0)
        queries = (joined_qkv[:, 0] + bias_query).astype(jnp.bfloat16).reshape(head_shape)
        keys_in = joined_qkv[:, 1].astype(jnp.bfloat16).reshape(head_shape)
        values_in = (joined_qkv[:, 2] + bias_value).astype(jnp.bfloat16).reshape(head_shape)
        heads_low, log_totals = attention_forward(queries, keys_in, values_in, seg_ids)
        attn_sum = summed_rows(heads_low, w_out, rows_dev)
        hidden, normed_a, inverse_a = layer_norm(
            stream + attn_sum + bias_all[1], gain_all[0], bias_all[2]
        )
        full_hidden = gather_rows(hidden.astype(jnp.bfloat16))
        up_shift = lax.dynamic_slice_in_dim(
            up_low.astype(jnp.float32), tp_rank * hidden_width, hidden_width, 0
        )
        pre_act = jnp.dot(full_hidden, w_up, preferred_element_type=jnp.float32) + up_shift
        act_low = gelu_exact(pre_act).astype(jnp.bfloat16)
        mlp_sum = summed_rows(act_low, w_down, rows_dev)
        stream, normed_b, inverse_b = layer_norm(
            hidden + mlp_sum + bias_all[3], gain_all[1], bias_all[4]
        )
        saved_acts.append(
            (
                full_in,
                queries,
                keys_in,
                values_in,
                log_totals,
                heads_low,
                normed_a,
                inverse_a,
                full_hidden,
                pre_act,
                act_low,
                normed_b,
                inverse_b,
                (w_in, w_out, w_up, w_down, gain_low),
            )
        )
    deviation = stream - teacher[0].astype(jnp.float32)
    count_all, square_all = lax.psum(
        (jnp.sum(weight_rows), jnp.sum(weight_rows[:, None] * deviation * deviation)),
        ("fsdp", "tp"),
    )
    loss = square_all / (count_all * width)
    token_total = length * lax.axis_size("fsdp")
    grad_rows = token_total / count_all * weight_rows[:, None] * deviation
    layer_grads_list = [None] * layers
    for layer_num in reversed(range(layers)):
        (
            full_in,
            queries,
            keys_in,
            values_in,
            log_totals,
            heads_low,
            normed_a,
            inverse_a,
            full_hidden,
            pre_act,
            act_low,
            normed_b,
            inverse_b,
            kept_weights,
        ) = saved_acts[layer_num]
        w_in, w_out, w_up, w_down, gain_low = (
            lax.all_gather(attn_in[layer_num], "fsdp", axis=0, tiled=True),
            lax.all_gather(attn_out[layer_num], "fsdp", axis=0, tiled=True),
            lax.all_gather(ff_in[layer_num], "fsdp", axis=0, tiled=True),
            lax.all_gather(ff_out[layer_num], "fsdp", axis=0, tiled=True),
            lax.all_gather(gains[layer_num], "fsdp", axis=1, tiled=True),
        )
        gain_all = gain_low.astype(jnp.float32)
        d_out = norm_back(grad_rows, normed_b, inverse_b, gain_all[1])
        gain_b_grad = jnp.sum(grad_rows * normed_b, axis=0)
        shift_b_grad = jnp.sum(grad_rows, axis=0)
        down_bias_grad = jnp.sum(d_out, axis=0)
        full_dout = gather_grads(d_out.astype(jnp.bfloat16))
        act_grad = jnp.dot(full_dout, w_down, preferred_element_type=jnp.float32)
        down_grad = outer_rows(full_dout, act_low)
        pre_grad = act_grad * gelu_slope(pre_act)
        up_bias_grad = jnp.sum(pre_grad, axis=0)
        pre_low = pre_grad.astype(jnp.bfloat16)
        up_grad = outer_rows(full_hidden, pre_low)
        hidden_grad = d_out + summed_grads(pre_low, w_up, rows_dev)
        d_mid = norm_back(hidden_grad, normed_a, inverse_a, gain_all[0])
        gain_a_grad = jnp.sum(hidden_grad * normed_a, axis=0)
        shift_a_grad = jnp.sum(hidden_grad, axis=0)
        out_bias_grad = jnp.sum(d_mid, axis=0)
        full_dmid = gather_grads(d_mid.astype(jnp.bfloat16))
        heads_grad = (
            jnp.dot(full_dmid, w_out, preferred_element_type=jnp.float32)
            .astype(jnp.bfloat16)
            .reshape(head_shape)
        )
        out_grad = outer_rows(full_dmid, heads_low)
        query_grad, key_grad, value_grad = attention_back(
            queries, keys_in, values_in, seg_ids, log_totals, heads_grad
        )
        qkv_low = (
            jnp.stack([query_grad, key_grad, value_grad], axis=1)
            .astype(jnp.bfloat16)
            .reshape(length, 3, heads_width)
        )
        qkv_sums = jnp.sum(qkv_low.astype(jnp.float32), axis=0)
        in_grad = outer_rows(full_in, qkv_low)
        grad_rows = d_mid + summed_grads(
            qkv_low.reshape(length, 3 * heads_width), w_in.reshape(width, 3 * heads_width), rows_dev
        )
        empty_row = jnp.zeros((width,), jnp.float32)
        bias_grad = jnp.stack(
            [
                lax.dynamic_update_slice_in_dim(empty_row, qkv_sums[2], tp_rank * heads_width, 0),
                out_bias_grad,
                shift_a_grad,
                down_bias_grad,
                shift_b_grad,
            ]
        )
        query_full = lax.dynamic_update_slice_in_dim(
            empty_row, qkv_sums[0], tp_rank * heads_width, 0
        )
        gain_grad = jnp.stack([gain_a_grad, gain_b_grad])
        up_bias_full = lax.dynamic_update_slice_in_dim(
            jnp.zeros((hidden_width * tp_count,), jnp.float32),
            up_bias_grad,
            tp_rank * hidden_width,
            0,
        )
        pieces_layer = (
            in_grad,
            out_grad,
            up_grad,
            down_grad,
            bias_grad,
            gain_grad,
            up_bias_full,
            query_full,
        )
        layer_grads_list[layer_num] = (
            lax.psum_scatter(pieces_layer[0], "fsdp", scatter_dimension=0, tiled=True),
            lax.psum_scatter(pieces_layer[1], "fsdp", scatter_dimension=0, tiled=True),
            lax.psum_scatter(pieces_layer[2], "fsdp", scatter_dimension=0, tiled=True),
            lax.psum_scatter(pieces_layer[3], "fsdp", scatter_dimension=0, tiled=True),
            lax.psum_scatter(pieces_layer[4], "fsdp", scatter_dimension=1, tiled=True),
            lax.psum_scatter(pieces_layer[5], "fsdp", scatter_dimension=1, tiled=True),
            lax.psum_scatter(pieces_layer[6], "fsdp", scatter_dimension=0, tiled=True),
            lax.psum_scatter(pieces_layer[7], "fsdp", scatter_dimension=0, tiled=True),
        )
    stacked = tuple(
        (
            jnp.stack([layer_entry[member] for layer_entry in layer_grads_list])
            for member in range(8)
        )
    )
    bias_shards, gain_shards, up_shards, query_shards = lax.psum(
        (stacked[4], stacked[5], stacked[6], stacked[7]), "tp"
    )
    return (
        stream.astype(jnp.bfloat16)[None],
        grad_rows[None],
        loss,
        stacked[0],
        stacked[1],
        stacked[2],
        stacked[3],
        bias_shards,
        gain_shards,
        up_shards,
        query_shards,
    )


def solution(mesh):
    in_specs = (
        P("fsdp", "tp", None),
        P("fsdp", None),
        P("fsdp", "tp"),
        P("fsdp", "tp", None),
        P(None, "fsdp", None, "tp"),
        P(None, "fsdp", "tp"),
        P(None, "fsdp", "tp"),
        P(None, "fsdp", "tp"),
        P(None, None, "fsdp"),
        P(None, None, "fsdp"),
        P(None, "fsdp"),
        P(None, "fsdp"),
    )
    out_specs = (
        P("fsdp", "tp", None),
        P("fsdp", "tp", None),
        P(),
        P(None, "fsdp", None, "tp"),
        P(None, "fsdp", "tp"),
        P(None, "fsdp", "tp"),
        P(None, "fsdp", "tp"),
        P(None, None, "fsdp"),
        P(None, None, "fsdp"),
        P(None, "fsdp"),
        P(None, "fsdp"),
    )
    return jax.shard_map(
        on_device, mesh=mesh, in_specs=in_specs, out_specs=out_specs, check_vma=False
    )
```

profile of v0, /device:TPU:0, one launch (start us, length us, event | category | flops | bytes accessed | tf_op | source)
XLA Modules:
  0.0 1511.8 jit_solution(7897830894833763545)
XLA Ops:
  14.0 63.2 %all-reduce.13 = (bf16[768]{0:T(1024)(128)(2,1)S(1)}, bf16[768]{0:T(1024)(128)(2,1)S(1)}, bf16[3072]{0:T(1024)(128)(2,1)S(1)}, bf16[3072]{0:T(1024)(128)(2,1)}) all-reduce(bf16[768]{0:T(1024)(128)(2,1)S(1)} %dynamic-update-slice, bf16[768]{0:T(1024)(128)(2,1)S(1)} %dynamic-update-slice.2, ...), channel_id=5, replica_groups=mesh['fsdp'=16,'tp'=2] {'fsdp'}, use_global_device_ids=true, to_apply=%add | all-reduce | flops 7680 | bytes 30720
  78.3 18.2 %all-gather.2 = bf16[1,5,768]{1,0,2:T(2,128)(2,1)S(1)} all-gather(bf16[1,5,48]{1,0,2:T(2,128)(2,1)S(1)} %copy.119), channel_id=4, replica_groups=mesh['fsdp'=16,'tp'=2] {'fsdp'}, dimensions={2}, use_global_device_ids=true | all-gather | bytes 8160 | tf_op jit(solution)/shard_map/all_gather | solution.py:197
  98.8 13.8 all-gather
  112.9 22.3 %all-gather.4 = bf16[1,768,384]{2,1,0:T(8,128)(2,1)} all-gather(bf16[1,48,384]{2,1,0:T(8,128)(2,1)S(1)} %get-tuple-element.233), channel_id=6, replica_groups=mesh['fsdp'=16,'tp'=2] {'fsdp'}, dimensions={1}, use_global_device_ids=true | all-gather | bytes 626688 | tf_op jit(solution)/shard_map/all_gather | solution.py:194
  135.3 2.6 copy.78
  137.9 2.8 fusion.34
  151.7 18.8 %all-gather.5 = bf16[1,2,768]{1,0,2:T(2,128)(2,1)S(1)} all-gather(bf16[1,2,48]{1,0,2:T(2,128)(2,1)S(1)} %copy.120), channel_id=7, replica_groups=mesh['fsdp'=16,'tp'=2] {'fsdp'}, dimensions={2}, use_global_device_ids=true | all-gather | bytes 3264 | tf_op jit(solution)/shard_map/all_gather | solution.py:198
  171.0 4.6 slice_reduce_fusion.7
  175.6 21.8 %slice_reduce_fusion.6 = (f32[768]{0:T(1024)S(1)}, f32[768]{0:T(1024)S(1)}, f32[768]{0:T(1024)S(1)}, f32[768]{0:T(1024)S(1)}) fusion(f32[1,5,768]{1,0,2:T(1,128)S(1)} %convert_element_type.299), kind=kLoop, calls=%fused_computation.163 | loop fusion | bytes 24576 | tf_op jit(solution)/shard_map/slice | solution.py:229
  201.2 12.1 all_gather.88
  213.2 5.1 multiply_convert_fusion.3
  218.3 33.3 %all-gather.28.cloned.1.call-done = bf16[1,768,1536]{2,1,0:T(8,128)(2,1)} async-done(((bf16[1,48,1536]{2,1,0:T(8,128)(2,1)}), bf16[1,768,1536]{2,1,0:T(8,128)(2,1)}) %all-gather.28.cloned.1.call-update) | async-done | bytes 2359312 | tf_op jit(solution)/shard_map/all_gather | solution.py:196
  251.6 4.4 fusion.39
  256.4 20.7 %all-gather.10 = bf16[1,5,768]{1,0,2:T(2,128)(2,1)S(1)} all-gather(bf16[1,5,48]{1,0,2:T(2,128)(2,1)S(1)} %copy.121), channel_id=12, replica_groups=mesh['fsdp'=16,'tp'=2] {'fsdp'}, dimensions={2}, use_global_device_ids=true | all-gather | bytes 8160 | tf_op jit(solution)/shard_map/all_gather | solution.py:197
  279.4 21.0 %all-gather.12 = bf16[1,768,384]{2,1,0:T(8,128)(2,1)} all-gather(bf16[1,48,384]{2,1,0:T(8,128)(2,1)S(1)} %get-tuple-element.232), channel_id=14, replica_groups=mesh['fsdp'=16,'tp'=2] {'fsdp'}, dimensions={1}, use_global_device_ids=true | all-gather | bytes 626688 | tf_op jit(solution)/shard_map/all_gather | solution.py:194
  300.3 3.9 copy.82
  304.2 11.3 reduce-scatter.29.cloned.1.call-done
  317.5 11.5 all_gather.92
  340.8 22.7 %all-gather.13 = bf16[1,2,768]{1,0,2:T(2,128)(2,1)S(1)} all-gather(bf16[1,2,48]{1,0,2:T(2,128)(2,1)S(1)} %copy.122), channel_id=15, replica_groups=mesh['fsdp'=16,'tp'=2] {'fsdp'}, dimensions={2}, use_global_device_ids=true | all-gather | bytes 3264 | tf_op jit(solution)/shard_map/all_gather | solution.py:198
  364.0 4.6 slice_reduce_fusion.1
  368.6 12.8 slice_reduce_fusion
  383.3 12.1 all_gather.98
  395.5 6.2 all-gather.32.cloned.1.call-done
  401.7 5.6 multiply_convert_fusion.2
  407.3 38.6 %all-gather.34.cloned.1.call-done = bf16[1,768,1536]{2,1,0:T(8,128)(2,1)} async-done(((bf16[1,48,1536]{2,1,0:T(8,128)(2,1)}), bf16[1,768,1536]{2,1,0:T(8,128)(2,1)}) %all-gather.34.cloned.1.call-update) | async-done | bytes 2359312 | tf_op jit(solution)/shard_map/all_gather | solution.py:196
  445.8 4.4 fusion.45
  451.0 39.0 %psum.42 = f32[]{:T(128)} all-reduce(f32[]{:T(128)} %get-tuple-element.213), channel_id=1, replica_groups=mesh['fsdp'=16,'tp'=2] {'fsdp','tp'}, use_global_device_ids=true, to_apply=%region_17.18 | all-reduce | flops 1 | bytes 8 | tf_op jit(solution)/shard_map/psum | solution.py:250
  492.5 2.5 multiply_reduce_fusion.2
  496.4 11.5 all_gather.102
  508.0 2.8 fusion.119
  511.9 2.3 fusion.42
  514.4 16.2 %reduce-scatter.35.cloned.1.call-done = bf16[256,768]{1,0:T(8,128)(2,1)} async-done(((bf16[512,768]{1,0:T(8,128)(2,1)}), bf16[256,768]{1,0:T(8,128)(2,1)}) %reduce-scatter.35.cloned.1.call-update) | async-done | bytes 393232 | tf_op jit(solution)/shard_map/reduce_scatter | solution.py:149
  530.5 2.4 multiply_reduce_fusion.3
  532.9 2.4 fusion.103
  535.3 11.8 all_gather.103
  547.7 4.3 fusion.52
  552.1 4.1 multiply_reduce_fusion.1
  556.2 4.7 multiply_convert_fusion.1
  565.9 17.5 %reduce-scatter.37.cloned.1.call-done = bf16[256,768]{1,0:T(8,128)(2,1)} async-done(((bf16[512,768]{1,0:T(8,128)(2,1)}), bf16[256,768]{1,0:T(8,128)(2,1)}) %reduce-scatter.37.cloned.1.call-update) | async-done | bytes 393232 | tf_op jit(solution)/shard_map/reduce_scatter | solution.py:149
  587.9 11.5 all_gather.104
  599.4 2.8 fusion.120
  627.4 2.6 multiply_reduce_fusion.5
  633.1 10.8 all_gather.105
  646.7 2.4 multiply_reduce_fusion
  658.7 2.7 fusion.122
  665.9 4.6 copy.97
  670.5 2.9 convolution_bitcast_fusion
  673.3 6.3 copy.92
  681.3 3.6 fusion.124
  686.5 3.7 fusion.123
  691.9 3.6 fusion.70
  697.1 3.6 fusion.67
  702.8 39.7 %psum.43 = f32[]{:T(128)} all-reduce(f32[]{:T(128)} %get-tuple-element.167), channel_id=1, replica_groups=mesh['fsdp'=16,'tp'=2] {'fsdp','tp'}, use_global_device_ids=true, to_apply=%region_33.34 | all-reduce | flops 1 | bytes 8 | tf_op jit(solution)/shard_map/psum | solution.py:250
  745.9 60.4 %all-reduce.10 = (f32[3072]{0:T(1024)S(1)}, f32[3072]{0:T(1024)S(1)}, f32[768]{0:T(1024)S(1)}, f32[768]{0:T(1024)S(1)}) all-reduce(f32[3072]{0:T(1024)S(1)} %dynamic_update_slice.38, f32[3072]{0:T(1024)S(1)} %dynamic_update_slice.37, f32[768]{0:T(1024)S(1)} %dynamic_update_slice.40, ...), channel_id=40, replica_groups=mesh['fsdp'=16,'tp'=2] {'fsdp'}, use_global_device_ids=true, to_apply=%region_65.66.clone | all-reduce | flops 7680 | bytes 61440
  807.5 49.6 %reduce-scatter.55.cloned.1.call-done = f32[48,5]{1,0:T(8,128)} async-done(((f32[768,5]{1,0:T(8,128)}), f32[48,5]{1,0:T(8,128)}) %reduce-scatter.55.cloned.1.call-update) | async-done | bytes 976
  857.9 8.6 all-reduce.12
  867.1 8.6 reduce-scatter.41.cloned.1.call-done
  877.7 59.9 %reduce-scatter.45.cloned.1.call-done = f32[48,384]{1,0:T(8,128)} async-done(((f32[768,384]{1,0:T(8,128)}), f32[48,384]{1,0:T(8,128)}) %reduce-scatter.45.cloned.1.call-update) | async-done | bytes 73744 | tf_op jit(solution)/shard_map/reduce_scatter | solution.py:351
  937.5 60.6 %reduce-scatter.43.cloned.1.call-done = f32[48,384]{1,0:T(8,128)} async-done(((f32[768,384]{1,0:T(8,128)}), f32[48,384]{1,0:T(8,128)}) %reduce-scatter.43.cloned.1.call-update) | async-done | bytes 73744 | tf_op jit(solution)/shard_map/reduce_scatter | solution.py:351
  999.7 186.4 %all-reduce.16.cloned.1.call-done = (f32[768,3,384]{2,1,0:T(4,128)}, f32[768,3,384]{2,1,0:T(4,128)}) async-done(((f32[768,3,384]{2,1,0:T(4,128)}, f32[768,3,384]{2,1,0:T(4,128)}), (f32[768,3,384]{2,1,0:T(4,128)}, f32[768,3,384]{2,1,0:T(4,128)})) %all-reduce.16.cloned.1.call-update) | async-done | bytes 7077904
  1188.9 77.1 %reduce-scatter.53.cloned.1.call-done = f32[48,1536]{1,0:T(8,128)} async-done(((f32[768,1536]{1,0:T(8,128)}), f32[48,1536]{1,0:T(8,128)}) %reduce-scatter.53.cloned.1.call-update) | async-done | bytes 294928 | tf_op jit(solution)/shard_map/reduce_scatter | solution.py:353
  1266.0 78.5 %reduce-scatter.51.cloned.1.call-done = f32[48,1536]{1,0:T(8,128)} async-done(((f32[768,1536]{1,0:T(8,128)}), f32[48,1536]{1,0:T(8,128)}) %reduce-scatter.51.cloned.1.call-update) | async-done | bytes 294928 | tf_op jit(solution)/shard_map/reduce_scatter | solution.py:353
  1346.4 76.9 %reduce-scatter.49.cloned.1.call-done = f32[48,1536]{1,0:T(8,128)} async-done(((f32[768,1536]{1,0:T(8,128)}), f32[48,1536]{1,0:T(8,128)}) %reduce-scatter.49.cloned.1.call-update) | async-done | bytes 294928 | tf_op jit(solution)/shard_map/reduce_scatter | solution.py:352
  1423.4 78.4 %reduce-scatter.47.cloned.1.call-done = f32[48,1536]{1,0:T(8,128)} async-done(((f32[768,1536]{1,0:T(8,128)}), f32[48,1536]{1,0:T(8,128)}) %reduce-scatter.47.cloned.1.call-update) | async-done | bytes 294928 | tf_op jit(solution)/shard_map/reduce_scatter | solution.py:352
  (412 shorter events, 124.2 us)
Async XLA Ops:
  7.2 105.4 %copy-start.59 = (s32[1,512]{1,0:T(1,128)S(1)}, s32[1,512]{1,0:T(1,128)}, u32[]{:S(2)}) copy-start(s32[1,512]{1,0:T(1,128)} %param.13) | copy-start | bytes 6148
  7.2 105.4 %copy-start.58 = (bf16[2,48,384]{2,1,0:T(8,128)(2,1)S(1)}, bf16[2,48,384]{2,1,0:T(8,128)(2,1)}, u32[]{:S(2)}) copy-start(bf16[2,48,384]{2,1,0:T(8,128)(2,1)} %param.17) | copy-start | bytes 221188
  7.2 128.1 %all-gather.24.cloned.1.call-start = ((), (), s32[]{:S(2)}) async-start(), calls=%async_computation.32 | async-start | bytes 1880064 | tf_op jit(solution)/shard_map/all_gather | solution.py:193
  8.9 188.5 %reduce-scatter.27.cloned.1.call-start = ((), (), s32[]{:S(2)}) async-start(), calls=%async_computation.18 | async-start | bytes 1179648 | tf_op jit(solution)/shard_map/reduce_scatter | solution.py:136
  98.1 45.4 %copy-start.70 = (f32[6,64]{1,0:T(8,128)}, f32[6,64]{1,0:T(8,128)S(1)}, u32[]{:S(2)}) copy-start(f32[6,64]{1,0:T(8,128)S(1)} %add.326) | copy-start | bytes 4612
  148.4 49.0 %copy-start.2 = (bf16[1,256,768]{2,1,0:T(8,128)(2,1)S(1)}, bf16[1,256,768]{2,1,0:T(8,128)(2,1)}, u32[]{:S(2)}) copy-start(bf16[1,256,768]{2,1,0:T(8,128)(2,1)} %param.12) | copy-start | bytes 1179652
  148.4 64.8 %all-gather.26.cloned.1.call-start = ((), (), s32[]{:S(2)}) async-start(), calls=%async_computation.33 | async-start | bytes 2506752 | tf_op jit(solution)/shard_map/all_gather | solution.py:195
  149.2 102.4 %all-gather.28.cloned.1.call-start = ((), (), s32[]{:S(2)}) async-start(), calls=%async_computation.34 | async-start | bytes 2506752 | tf_op jit(solution)/shard_map/all_gather | solution.py:196
  150.0 150.3 %all-gather.30.cloned.1.call-start = ((), (), s32[]{:S(2)}) async-start(), calls=%async_computation.35 | async-start | bytes 1880064 | tf_op jit(solution)/shard_map/all_gather | solution.py:193
  150.6 164.9 %reduce-scatter.29.cloned.1.call-start = ((), (), s32[]{:S(2)}) async-start(), calls=%async_computation.19 | async-start | bytes 1179648 | tf_op jit(solution)/shard_map/reduce_scatter | solution.py:136
  198.6 116.9 %copy-start.60 = (f32[256]{0:T(256)}, f32[256]{0:T(256)S(1)}, u32[]{:S(2)}) copy-start(f32[256]{0:T(256)S(1)} %broadcast_multiply_fusion.12) | copy-start | bytes 3076
  199.9 115.6 %copy-start.64 = (f32[256]{0:T(256)}, f32[256]{0:T(256)S(1)}, u32[]{:S(2)}) copy-start(f32[256]{0:T(256)S(1)} %add_rsqrt_fusion.3) | copy-start | bytes 3076
  213.2 5.1 copy-start.19
  256.1 59.5 %copy-start.3 = (bf16[256,768]{1,0:T(8,128)(2,1)S(1)}, bf16[256,768]{1,0:T(8,128)(2,1)}, u32[]{:S(2)}) copy-start(bf16[256,768]{1,0:T(8,128)(2,1)} %reduce-scatter.27.cloned.1.call-done) | copy-start | bytes 1179652
  256.1 125.4 %reduce-scatter.31.cloned.1.call-start = ((), (), s32[]{:S(2)}) async-start(), calls=%async_computation.20 | async-start | bytes 1179648 | tf_op jit(solution)/shard_map/reduce_scatter | solution.py:136
  279.4 54.5 %copy-start.72 = (f32[6,64]{1,0:T(8,128)}, f32[6,64]{1,0:T(8,128)S(1)}, u32[]{:S(2)}) copy-start(f32[6,64]{1,0:T(8,128)S(1)} %add.352) | copy-start | bytes 4612
  315.5 14.5 copy-start.6
  317.1 64.4 %copy-start.62 = (f32[256]{0:T(256)}, f32[256]{0:T(256)S(1)}, u32[]{:S(2)}) copy-start(f32[256]{0:T(256)S(1)} %broadcast_multiply_fusion.11) | copy-start | bytes 3076
  317.3 64.1 %copy-start.65 = (f32[256]{0:T(256)}, f32[256]{0:T(256)S(1)}, u32[]{:S(2)}) copy-start(f32[256]{0:T(256)S(1)} %add_rsqrt_fusion.2) | copy-start | bytes 3076
  335.2 5.1 copy-start.17
  337.2 26.8 %copy-start.80 = (bf16[3072]{0:T(1024)(128)(2,1)S(1)}, bf16[3072]{0:T(1024)(128)(2,1)}, u32[]{:S(2)}) copy-start(bf16[3072]{0:T(1024)(128)(2,1)} %get-tuple-element.204) | copy-start | bytes 18436
  338.7 63.0 %all-gather.32.cloned.1.call-start = ((), (), s32[]{:S(2)}) async-start(), calls=%async_computation.36 | async-start | bytes 2506752 | tf_op jit(solution)/shard_map/all_gather | solution.py:195
  339.5 106.4 %all-gather.34.cloned.1.call-start = ((), (), s32[]{:S(2)}) async-start(), calls=%async_computation.37 | async-start | bytes 2506752 | tf_op jit(solution)/shard_map/all_gather | solution.py:196
  340.2 150.6 %reduce-scatter.33.cloned.1.call-start = ((), (), s32[]{:S(2)}) async-start(), calls=%async_computation.21 | async-start | bytes 1179648 | tf_op jit(solution)/shard_map/reduce_scatter | solution.py:136
  445.8 4.5 copy-start.83
  450.3 80.2 %reduce-scatter.35.cloned.1.call-start = ((), (), s32[]{:S(2)}) async-start(), calls=%async_computation.22 | async-start | bytes 1179648 | tf_op jit(solution)/shard_map/reduce_scatter | solution.py:149
  492.2 15.7 %copy-start.87 = (bf16[1,768,1536]{2,1,0:T(8,128)(2,1)S(1)}, bf16[1,768,1536]{2,1,0:T(8,128)(2,1)}, u32[]{:S(2)}) copy-start(bf16[1,768,1536]{2,1,0:T(8,128)(2,1)} %all-gather.34.cloned.1.call-done) | copy-start | bytes 7077892
  492.3 15.7 %copy-start.89 = (f32[512,1536]{1,0:T(8,128)S(1)}, f32[512,1536]{1,0:T(8,128)}, u32[]{:S(2)}) copy-start(f32[512,1536]{1,0:T(8,128)} %get-tuple-element.253) | copy-start | bytes 9437188
  514.3 69.1 %reduce-scatter.37.cloned.1.call-start = ((), (), s32[]{:S(2)}) async-start(), calls=%async_computation.23 | async-start | bytes 1179648 | tf_op jit(solution)/shard_map/reduce_scatter | solution.py:149
  530.5 16.6 %copy-start.37 = (bf16[1,768,384]{2,1,0:T(8,128)(2,1)S(1)}, bf16[1,768,384]{2,1,0:T(8,128)(2,1)}, u32[]{:S(2)}) copy-start(bf16[1,768,384]{2,1,0:T(8,128)(2,1)} %all-gather.12) | copy-start | bytes 1769476
  535.3 16.7 %slice-start.2 = ((s8[6291456]{0:T(1024)(128)(4,1)}), s8[4194304]{0:T(1024)(128)(4,1)S(1)}, s32[]{:S(2)}) async-start(s8[6291456]{0:T(1024)(128)(4,1)} %bitcast.236), calls=%async_computation.45 | async-start | bytes 8388608
  547.1 4.9 copy-start.26
  552.1 10.7 copy-start.50
  556.2 4.8 copy-start.11
  562.8 20.7 %copy-start.14 = (f32[256,768]{1,0:T(8,128)S(1)}, f32[256,768]{1,0:T(8,128)}, u32[]{:S(2)}) copy-start(f32[256,768]{1,0:T(8,128)} %get-tuple-element.210) | copy-start | bytes 2359300
  562.8 20.7 %copy-start.63 = (f32[256]{0:T(256)S(1)}, f32[256]{0:T(256)}, u32[]{:S(2)}) copy-start(f32[256]{0:T(256)} %copy-done.62) | copy-start | bytes 3076
  562.8 20.6 %copy-start.66 = (f32[256]{0:T(256)S(1)}, f32[256]{0:T(256)}, u32[]{:S(2)}) copy-start(f32[256]{0:T(256)} %copy-done.65) | copy-start | bytes 3076
  565.9 61.5 %reduce-scatter.39.cloned.1.call-start = ((), (), s32[]{:S(2)}) async-start(), calls=%async_computation.24 | async-start | bytes 1179648 | tf_op jit(solution)/shard_map/reduce_scatter | solution.py:149
  583.4 15.9 %copy-start.85 = (bf16[1,768,1536]{2,1,0:T(8,128)(2,1)S(1)}, bf16[1,768,1536]{2,1,0:T(8,128)(2,1)}, u32[]{:S(2)}) copy-start(bf16[1,768,1536]{2,1,0:T(8,128)(2,1)} %all-gather.28.cloned.1.call-done) | copy-start | bytes 7077892
  583.4 15.9 %copy-start.88 = (f32[512,1536]{1,0:T(8,128)S(1)}, f32[512,1536]{1,0:T(8,128)}, u32[]{:S(2)}) copy-start(f32[512,1536]{1,0:T(8,128)} %get-tuple-element.249) | copy-start | bytes 9437188
  605.7 21.7 %copy-start.61 = (f32[256]{0:T(256)S(1)}, f32[256]{0:T(256)}, u32[]{:S(2)}) copy-start(f32[256]{0:T(256)} %copy-done.60) | copy-start | bytes 3076
  605.7 138.1 %reduce-scatter.61.cloned.1.call-start = ((), (), s32[]{:S(2)}) async-start(), calls=%async_computation.41 | async-start | bytes 417792
  607.6 36.9 %slice-start = ((s8[6291456]{0:T(1024)(128)(4,1)}), s8[2097152]{0:T(1024)(128)(4,1)S(1)}, s32[]{:S(2)}) async-start(s8[6291456]{0:T(1024)(128)(4,1)} %bitcast.234), calls=%async_computation.43 | async-start | bytes 4194304
  615.2 129.7 %reduce-scatter.57.cloned.1.call-start = ((), (), s32[]{:S(2)}) async-start(), calls=%async_computation.39 | async-start | bytes 417792
  627.3 179.4 %reduce-scatter.59.cloned.1.call-start = ((), (), s32[]{:S(2)}) async-start(), calls=%async_computation.40 | async-start | bytes 417792
  627.4 16.6 %copy-start.35 = (bf16[1,768,384]{2,1,0:T(8,128)(2,1)S(1)}, bf16[1,768,384]{2,1,0:T(8,128)(2,1)}, u32[]{:S(2)}) copy-start(bf16[1,768,384]{2,1,0:T(8,128)(2,1)} %all-gather.4) | copy-start | bytes 1769476
  627.4 17.1 %slice-start.1 = ((s8[6291456]{0:T(1024)(128)(4,1)}), s8[4194304]{0:T(1024)(128)(4,1)S(1)}, s32[]{:S(2)}) async-start(s8[6291456]{0:T(1024)(128)(4,1)} %bitcast.234), calls=%async_computation.44 | async-start | bytes 8388608
  630.0 14.5 copy-start.57
  653.8 203.3 %reduce-scatter.55.cloned.1.call-start = ((), (), s32[]{:S(2)}) async-start(), calls=%async_computation.38 | async-start | bytes 417792
  655.2 220.5 %reduce-scatter.41.cloned.1.call-start = ((), (), s32[]{:S(2)}) async-start(), calls=%async_computation.25 | async-start | bytes 1179648 | tf_op jit(solution)/shard_map/reduce_scatter | solution.py:149
  658.6 4.9 copy-start.51
  658.7 278.9 %reduce-scatter.45.cloned.1.call-start = ((), (), s32[]{:S(2)}) async-start(), calls=%async_computation.27 | async-start | bytes 1253376 | tf_op jit(solution)/shard_map/reduce_scatter | solution.py:351
  661.5 336.6 %reduce-scatter.43.cloned.1.call-start = ((), (), s32[]{:S(2)}) async-start(), calls=%async_computation.26 | async-start | bytes 1253376 | tf_op jit(solution)/shard_map/reduce_scatter | solution.py:351
  663.2 522.8 %all-reduce.16.cloned.1.call-start = ((), (), s32[]{:S(2)}) async-start(), calls=%async_computation.42 | async-start | bytes 18874368
  665.9 4.6 copy-start.49
  665.9 4.6 copy-start.52
  679.7 586.3 %reduce-scatter.53.cloned.1.call-start = ((), (), s32[]{:S(2)}) async-start(), calls=%async_computation.31 | async-start | bytes 5013504 | tf_op jit(solution)/shard_map/reduce_scatter | solution.py:353
  684.9 659.6 %reduce-scatter.51.cloned.1.call-start = ((), (), s32[]{:S(2)}) async-start(), calls=%async_computation.30 | async-start | bytes 5013504 | tf_op jit(solution)/shard_map/reduce_scatter | solution.py:353
  690.2 733.1 %reduce-scatter.49.cloned.1.call-start = ((), (), s32[]{:S(2)}) async-start(), calls=%async_computation.29 | async-start | bytes 5013504 | tf_op jit(solution)/shard_map/reduce_scatter | solution.py:352
  695.5 806.3 %reduce-scatter.47.cloned.1.call-start = ((), (), s32[]{:S(2)}) async-start(), calls=%async_computation.28 | async-start | bytes 5013504 | tf_op jit(solution)/shard_map/reduce_scatter | solution.py:352
  700.7 42.5 %copy-start.78 = (f32[1536]{0:T(1024)S(1)}, f32[1536]{0:T(1024)}, u32[]{:S(2)}) copy-start(f32[1536]{0:T(1024)} %get-tuple-element.258) | copy-start | bytes 18436
  700.7 42.8 %copy-start.77 = (f32[384]{0:T(512)S(1)}, f32[384]{0:T(512)}, u32[]{:S(2)}) copy-start(f32[384]{0:T(512)} %get-tuple-element.236) | copy-start | bytes 4612
  700.7 43.9 %copy-start.79 = (f32[1536]{0:T(1024)S(1)}, f32[1536]{0:T(1024)}, u32[]{:S(2)}) copy-start(f32[1536]{0:T(1024)} %get-tuple-element.260) | copy-start | bytes 18436
  700.7 175.0 %copy-start.13 = (f32[256,768]{1,0:T(8,128)S(1)}, f32[256,768]{1,0:T(8,128)}, u32[]{:S(2)}) copy-start(f32[256,768]{1,0:T(8,128)} %copy-done.12) | copy-start | bytes 2359300
  (55 other events, 125.0 us)
Sparse Core Ops, SparseCore 0:
  10.9 43.1 all-gather.23
  148.5 13.6 reduce-scatter.26
  165.4 42.2 all-gather.25
  210.6 40.9 all-gather.27
  254.6 41.9 all-gather.29
  299.3 16.1 reduce-scatter.28
  338.8 17.4 reduce-scatter.30
  359.4 42.2 all-gather.31
  404.8 40.9 all-gather.33
  450.4 16.7 reduce-scatter.32
  514.4 16.0 reduce-scatter.34
  566.0 17.4 reduce-scatter.36
  605.8 17.4 reduce-scatter.38
  627.1 55.5 reduce-scatter.60
  686.0 54.6 reduce-scatter.56
  744.5 54.5 reduce-scatter.58
  802.4 54.6 reduce-scatter.54
  859.3 16.3 reduce-scatter.40
  879.3 58.1 reduce-scatter.44
  941.0 57.0 reduce-scatter.42
  1001.8 184.1 all-reduce.15
  1190.4 75.5 reduce-scatter.52
  1269.9 74.5 reduce-scatter.50
  1348.7 74.5 reduce-scatter.48
  1427.2 74.5 reduce-scatter.46
where the time goes:
time: 1520 us; the launch traced here: 1510 us
  waiting for transfers between devices  802 us (53%)
  blocking collectives  430 us (28%)
  local copies, waits for them, and re-layouts  116 us (8%)
  matrix products  88.7 us (6%)
  other arithmetic  52.2 us (3%)
  between operations  21.8 us (1%)
    unnamed x30, waiting for transfers between devices  238 us
    reduce_scatter x2, waiting for transfers between devices, on_device(): lax.psum_scatter(pieces_layer[3], 'fsdp', scatter_dimension=0, tiled=True)  156 us
    reduce_scatter x2, waiting for transfers between devices, on_device(): lax.psum_scatter(pieces_layer[2], 'fsdp', scatter_dimension=0, tiled=True)  155 us
    unnamed x2, blocking collectives  124 us
    reduce_scatter x2, waiting for transfers between devices, on_device(): lax.psum_scatter(pieces_layer[1], 'fsdp', scatter_dimension=0, tiled=True)  120 us
    psum x2, blocking collectives, on_device(): lax.psum((jnp.sum(weight_rows), jnp.sum(weight_rows[:, None] * deviation...  78.8 us
    all_gather x2, waiting for transfers between devices, on_device(): lax.all_gather(ff_out[layer_num], 'fsdp', axis=0, tiled=True)  71.9 us
    all_gather x4, blocking collectives, gather_rows(): return lax.all_gather(values_low, 'tp', axis=0, tiled=True)  49.6 us
  transfers between devices with their start and end apart: 25, of which 15 were waited for; matrix products, arithmetic and copies ran while one was open for 11% of the time, Pallas kernels for 0%

commit v1 on v0

--- a/solution.py
+++ b/solution.py
@@ -1,9 +1,149 @@
+import functools
+
 import jax
 import jax.numpy as jnp
 from jax import lax
+from jax.experimental import pallas as pl
+from jax.experimental.pallas import tpu as pltpu
 from jax.sharding import PartitionSpec as P
 
 HEAD_DIM = 64
+MESH = pl.DeviceIdType.MESH
+PIECE = 384
+
+
+def group_place(extra):
+    spot = lax.axis_index("fsdp") // extra
+    return spot // 4, (spot // 2) % 2, spot % 2
+
+
+def group_peer(extra, row, col, core):
+    rest = lax.axis_index("fsdp") % extra
+    return {"fsdp": ((row * 2 + col) * 2 + core) * extra + rest, "tp": lax.axis_index("tp")}
+
+
+def gather_kernel(extra, pieces, own_ref, full_ref, z_send, z_recv, hop_send, hop_recv, local_sem):
+    z, y, c = group_place(extra)
+    z_peers = [group_peer(extra, (z + step) % 4, y, c) for step in (1, 2, 3)]
+    y_peer = group_peer(extra, z, 1 - y, c)
+    c_peer = group_peer(extra, z, y, 1 - c)
+    barrier = pltpu.get_barrier_semaphore()
+    for peer in (*z_peers, y_peer, c_peer):
+        pl.semaphore_signal(barrier, inc=1, device_id=peer, device_id_type=MESH)
+    pl.semaphore_wait(barrier, 5)
+
+    def z_copy(piece, step):
+        return pltpu.make_async_remote_copy(
+            src_ref=own_ref.at[piece],
+            dst_ref=full_ref.at[piece, z, y, c],
+            send_sem=z_send.at[piece, step],
+            recv_sem=z_recv.at[piece, step],
+            device_id=z_peers[step],
+            device_id_type=MESH,
+        )
+
+    def own_copy(piece):
+        return pltpu.make_async_copy(own_ref.at[piece], full_ref.at[piece, z, y, c], local_sem.at[piece])
+
+    def hop_copy(piece, kind):
+        column = 1 - y if kind == 2 else y
+        return pltpu.make_async_remote_copy(
+            src_ref=full_ref.at[piece, :, column, c],
+            dst_ref=full_ref.at[piece, :, column, c],
+            send_sem=hop_send.at[piece, kind],
+            recv_sem=hop_recv.at[piece, kind],
+            device_id=y_peer if kind == 0 else c_peer,
+            device_id_type=MESH,
+        )
+
+    def issue(piece, carry):
+        own_copy(piece).start()
+        for step in range(3):
+            z_copy(piece, step).start()
+        return carry
+
+    lax.fori_loop(0, pieces, issue, 0)
+
+    def forward(step, carry):
+        @pl.when(step < pieces)
+        def _():
+            own_copy(step).wait()
+            for k in range(3):
+                z_copy(step, k).wait_recv()
+            hop_copy(step, 0).start()
+            hop_copy(step, 1).start()
+
+        @pl.when(step > 0)
+        def _():
+            hop_copy(step - 1, 0).wait_recv()
+            hop_copy(step - 1, 2).start()
+
+        return carry
+
+    lax.fori_loop(0, pieces + 1, forward, 0)
+
+    def finish(piece, carry):
+        hop_copy(piece, 1).wait_recv()
+        hop_copy(piece, 2).wait_recv()
+        for k in range(3):
+            z_copy(piece, k).wait_send()
+            hop_copy(piece, k).wait_send()
+        return carry
+
+    lax.fori_loop(0, pieces, finish, 0)
+
+
+def gather_all(own, extra):
+    pieces, rows, cols = own.shape
+    return pl.pallas_call(
+        functools.partial(gather_kernel, extra, pieces),
+        out_shape=jax.ShapeDtypeStruct((pieces, 4, 2, 2, rows, cols), own.dtype),
+        in_specs=[pl.BlockSpec(memory_space=pl.ANY)],
+        out_specs=pl.BlockSpec(memory_space=pltpu.VMEM),
+        scratch_shapes=[
+            pltpu.SemaphoreType.DMA((pieces, 3)),
+            pltpu.SemaphoreType.DMA((pieces, 3)),
+            pltpu.SemaphoreType.DMA((pieces, 3)),
+            pltpu.SemaphoreType.DMA((pieces, 3)),
+            pltpu.SemaphoreType.DMA((pieces,)),
+        ],
+        compiler_params=pltpu.CompilerParams(
+            collective_id=0, has_side_effects=True, vmem_limit_bytes=40 * 1024 * 1024
+        ),
+        name="gather_weights",
+    )(own)
+
+
+def shard_pieces(shard):
+    layers, rows = shard.shape[0], shard.shape[1]
+    return jnp.swapaxes(shard.reshape(layers, rows, -1, PIECE), 1, 2)
+
+
+def widen(shard, extra):
+    if extra == 1:
+        return shard
+    size = lax.axis_size("fsdp")
+    groups = [list(range(first, first + extra)) for first in range(0, size, extra)]
+    return lax.all_gather(shard, "fsdp", axis=1, axis_index_groups=groups, tiled=True)
+
+
+def fetch_matrices(attn_in, attn_out, ff_in, ff_out):
+    extra = lax.axis_size("fsdp") // 16
+    layers = attn_in.shape[0]
+    stacked = jnp.concatenate(
+        [shard_pieces(widen(part, extra)) for part in (attn_in, attn_out, ff_in, ff_out)], axis=1
+    )
+    per_layer, rows = stacked.shape[1], stacked.shape[2]
+    full = gather_all(stacked.reshape(layers * per_layer, rows, PIECE), extra)
+    full = full.reshape(layers, per_layer, 16 * rows, PIECE)
+    counts = [part.size // layers // (part.shape[1] * PIECE) for part in (attn_in, attn_out, ff_in, ff_out)]
+    joined, start = [], 0
+    for count in counts:
+        block = full[:, start : start + count]
+        joined.append(jnp.swapaxes(block, 1, 2).reshape(layers, 16 * rows, count * PIECE))
+        start += count
+    joined[0] = joined[0].reshape(layers, 16 * rows, 3, -1)
+    return joined
 
 
 epsilon = 1e-05
@@ -188,12 +328,15 @@
     weight_rows = (valid[0] * (own_seg > 0).astype(jnp.int32)).astype(jnp.float32)
     stream = tokens[0].astype(jnp.float32)
     saved_acts = []
+    full_attn_in, full_attn_out, full_ff_in, full_ff_out = fetch_matrices(
+        attn_in, attn_out, ff_in, ff_out
+    )
     for layer_num in range(layers):
         fetched = (
-            lax.all_gather(attn_in[layer_num], "fsdp", axis=0, tiled=True),
-            lax.all_gather(attn_out[layer_num], "fsdp", axis=0, tiled=True),
-            lax.all_gather(ff_in[layer_num], "fsdp", axis=0, tiled=True),
-            lax.all_gather(ff_out[layer_num], "fsdp", axis=0, tiled=True),
+            full_attn_in[layer_num],
+            full_attn_out[layer_num],
+            full_ff_in[layer_num],
+            full_ff_out[layer_num],
             lax.all_gather(biases[layer_num], "fsdp", axis=1, tiled=True),
             lax.all_gather(gains[layer_num], "fsdp", axis=1, tiled=True),
             lax.all_gather(ff_bias[layer_num], "fsdp", axis=0, tiled=True),
@@ -272,13 +415,7 @@
             inverse_b,
             kept_weights,
         ) = saved_acts[layer_num]
-        w_in, w_out, w_up, w_down, gain_low = (
-            lax.all_gather(attn_in[layer_num], "fsdp", axis=0, tiled=True),
-            lax.all_gather(attn_out[layer_num], "fsdp", axis=0, tiled=True),
-            lax.all_gather(ff_in[layer_num], "fsdp", axis=0, tiled=True),
-            lax.all_gather(ff_out[layer_num], "fsdp", axis=0, tiled=True),
-            lax.all_gather(gains[layer_num], "fsdp", axis=1, tiled=True),
-        )
+        w_in, w_out, w_up, w_down, gain_low = kept_weights
         gain_all = gain_low.astype(jnp.float32)
         d_out = norm_back(grad_rows, normed_b, inverse_b, gain_all[1])
         gain_b_grad = jnp.sum(grad_rows * normed_b, axis=0)

time: 1520 us -> 1520 us (level)
  Pallas kernels: 0 us -> 111 us
  waiting for transfers between devices: 802 us -> 723 us
  blocking collectives: 430 us -> 383 us
  local copies, waits for them, and re-layouts: 116 us -> 140 us
    pallas_call x0 -> x1, Pallas kernels: none -> 111 us  [gather_all(): pl.pallas_call(functools.partial(gather_kernel, extra, pieces), out_shape...]
    all_gather x6 -> x0, waiting for transfers between devices: 78.1 us -> none  [the longest x2 71.9 us: on_device(): lax.all_gather(ff_out[layer_num], 'fsdp', axis=0, tiled=True)]
    all_gather x2 -> x0, blocking collectives: 43.3 us -> none  [on_device(): lax.all_gather(attn_out[layer_num], 'fsdp', axis=0, tiled=True)]
    unnamed x215 -> x230, local copies, waits for them, and re-layouts: 28.4 us -> 47.8 us
    slice x4 -> x5, local copies, waits for them, and re-layouts: 3.12 us -> 22 us  [the longest x2 13 us: fetch_matrices(): block = full[:, start:start + count]]
    unnamed x30 -> x24, waiting for transfers between devices: 238 us -> 233 us
  transfers between devices with their start and end apart: 25 -> 19, of which waited for: 15 -> 12; matrix products, arithmetic and copies ran while one was open for 11% -> 11% of each run, Pallas kernels for 0% -> 0%
where the time goes in v1:
time: 1520 us
  waiting for transfers between devices  723 us (48%)
  blocking collectives  383 us (25%)
  local copies, waits for them, and re-layouts  140 us (9%)
  Pallas kernels  111 us (7%)
  matrix products  83.3 us (5%)
  other arithmetic  55.5 us (4%)
  between operations  21.6 us (1%)
    unnamed x24, waiting for transfers between devices  233 us
    reduce_scatter x2, waiting for transfers between devices, on_device(): lax.psum_scatter(pieces_layer[2], 'fsdp', scatter_dimension=0, tiled=True)  155 us
    reduce_scatter x2, waiting for transfers between devices, on_device(): lax.psum_scatter(pieces_layer[3], 'fsdp', scatter_dimension=0, tiled=True)  155 us
    unnamed x2, blocking collectives  123 us
    reduce_scatter x2, waiting for transfers between devices, on_device(): lax.psum_scatter(pieces_layer[1], 'fsdp', scatter_dimension=0, tiled=True)  120 us
    pallas_call x1, Pallas kernels, gather_all(): pl.pallas_call(functools.partial(gather_kernel, extra, pieces), out_shape...  111 us
    psum x2, blocking collectives, on_device(): lax.psum((jnp.sum(weight_rows), jnp.sum(weight_rows[:, None] * deviation...  76.7 us
    all_gather x4, blocking collectives, gather_rows(): return lax.all_gather(values_low, 'tp', axis=0, tiled=True)  50.4 us
  transfers between devices with their start and end apart: 19, of which 12 were waited for; matrix products, arithmetic and copies ran while one was open for 11% of the time, Pallas kernels for 0%

profile of v1, /device:TPU:0, one launch (start us, length us, event | category | flops | bytes accessed | tf_op | source)
XLA Modules:
  0.0 1517.9 jit_solution(14179008785488560701)
XLA Ops:
  7.2 14.7 all-gather
  24.2 110.6 %gather_weights.1 = bf16[24,4,2,2,48,384]{5,4,3,2,1,0:T(8,128)(2,1)} custom-call(bf16[24,48,384]{2,1,0:T(8,128)(2,1)S(1)} %bitcast.225), custom_call_target="tpu_custom_call" | custom-call | tf_op jit(solution)/shard_map/gather_weights/pallas_call | solution.py:98
  134.8 4.1 slice.201
  138.9 4.3 copy.134
  151.5 62.3 %all-reduce.13 = (bf16[768]{0:T(1024)(128)(2,1)S(1)}, bf16[768]{0:T(1024)(128)(2,1)}, bf16[3072]{0:T(1024)(128)(2,1)}, bf16[3072]{0:T(1024)(128)(2,1)}) all-reduce(bf16[768]{0:T(1024)(128)(2,1)S(1)} %dynamic-update-slice, bf16[768]{0:T(1024)(128)(2,1)S(1)} %dynamic-update-slice.2, ...), channel_id=4, replica_groups=mesh['fsdp'=16,'tp'=2] {'fsdp'}, use_global_device_ids=true, to_apply=%add | all-reduce | flops 7680 | bytes 30720
  214.2 18.3 %all-gather.5 = bf16[1,5,768]{1,0,2:T(2,128)(2,1)S(1)} all-gather(bf16[1,5,48]{1,0,2:T(2,128)(2,1)S(1)} %copy.139), channel_id=7, replica_groups=mesh['fsdp'=16,'tp'=2] {'fsdp'}, dimensions={2}, use_global_device_ids=true | all-gather | bytes 8160 | tf_op jit(solution)/shard_map/all_gather | solution.py:340
  232.4 20.6 %all-gather.1 = bf16[1,5,768]{1,0,2:T(2,128)(2,1)S(1)} all-gather(bf16[1,5,48]{1,0,2:T(2,128)(2,1)S(1)} %copy.135), channel_id=3, replica_groups=mesh['fsdp'=16,'tp'=2] {'fsdp'}, dimensions={2}, use_global_device_ids=true | all-gather | bytes 8160 | tf_op jit(solution)/shard_map/all_gather | solution.py:340
  262.8 2.7 convolution_convert_fusion.7
  266.0 8.9 fusion.82
  275.0 18.5 %all-gather.3 = bf16[1,2,768]{1,0,2:T(2,128)(2,1)S(1)} all-gather(bf16[1,2,48]{1,0,2:T(2,128)(2,1)S(1)} %copy.136), channel_id=5, replica_groups=mesh['fsdp'=16,'tp'=2] {'fsdp'}, dimensions={2}, use_global_device_ids=true | all-gather | bytes 3264 | tf_op jit(solution)/shard_map/all_gather | solution.py:341
  294.0 6.6 copy.138
  300.6 7.0 copy.137
  307.7 4.5 slice_reduce_fusion.7
  312.3 12.6 slice_reduce_fusion.6
  324.9 5.0 fusion.83
  329.9 2.5 fusion.84
  336.3 12.0 all_gather.52
  348.3 3.0 multiply_convert_fusion.3
  355.1 14.7 reduce-scatter.29.cloned.1.call-done
  371.9 11.5 all_gather.54
  391.5 2.7 convolution_convert_fusion.6
  394.8 22.6 %all-gather.7 = bf16[1,2,768]{1,0,2:T(2,128)(2,1)S(1)} all-gather(bf16[1,2,48]{1,0,2:T(2,128)(2,1)S(1)} %copy.140), channel_id=9, replica_groups=mesh['fsdp'=16,'tp'=2] {'fsdp'}, dimensions={2}, use_global_device_ids=true | all-gather | bytes 3264 | tf_op jit(solution)/shard_map/all_gather | solution.py:341
  417.9 4.6 slice_reduce_fusion.1
  422.5 12.7 slice_reduce_fusion
  437.3 12.0 all_gather.58
  449.3 3.0 multiply_convert_fusion.2
  456.5 37.1 %psum.42 = f32[]{:T(128)} all-reduce(f32[]{:T(128)} %get-tuple-element.213), channel_id=1, replica_groups=mesh['fsdp'=16,'tp'=2] {'fsdp','tp'}, use_global_device_ids=true, to_apply=%region_17.18 | all-reduce | flops 1 | bytes 8 | tf_op jit(solution)/shard_map/psum | solution.py:393
  496.0 2.6 multiply_reduce_fusion.2
  500.0 10.9 all_gather.60
  510.9 2.8 fusion.91
  514.9 2.3 convolution_convert_fusion.1
  517.3 18.0 %reduce-scatter.35.cloned.1.call-done = bf16[256,768]{1,0:T(8,128)(2,1)} async-done(((bf16[512,768]{1,0:T(8,128)(2,1)}), bf16[256,768]{1,0:T(8,128)(2,1)}) %reduce-scatter.35.cloned.1.call-update) | async-done | bytes 393232 | tf_op jit(solution)/shard_map/reduce_scatter | solution.py:289
  537.6 2.4 fusion.75
  540.0 11.8 all_gather.61
  553.7 4.3 fusion.26
  558.1 4.2 multiply_reduce_fusion.1
  562.3 4.7 multiply_convert_fusion.1
  572.0 17.5 %reduce-scatter.37.cloned.1.call-done = bf16[256,768]{1,0:T(8,128)(2,1)} async-done(((bf16[512,768]{1,0:T(8,128)(2,1)}), bf16[256,768]{1,0:T(8,128)(2,1)}) %reduce-scatter.37.cloned.1.call-update) | async-done | bytes 393232 | tf_op jit(solution)/shard_map/reduce_scatter | solution.py:289
  593.9 11.5 all_gather.62
  605.5 2.8 fusion.92
  636.4 2.6 multiply_reduce_fusion.5
  642.1 10.7 all_gather.63
  656.9 2.4 multiply_reduce_fusion
  669.0 2.7 fusion.94
  673.7 2.3 fusion.37
  676.1 4.6 copy.112
  680.6 2.9 convolution_bitcast_fusion
  683.5 6.4 copy.107
  691.5 3.6 fusion.96
  696.8 3.7 fusion.95
  702.1 3.6 fusion.45
  707.4 3.6 fusion.42
  713.0 39.6 %psum.43 = f32[]{:T(128)} all-reduce(f32[]{:T(128)} %get-tuple-element.167), channel_id=1, replica_groups=mesh['fsdp'=16,'tp'=2] {'fsdp','tp'}, use_global_device_ids=true, to_apply=%region_33.34 | all-reduce | flops 1 | bytes 8 | tf_op jit(solution)/shard_map/psum | solution.py:393
  756.0 60.3 %all-reduce.10 = (f32[3072]{0:T(1024)S(1)}, f32[3072]{0:T(1024)S(1)}, f32[768]{0:T(1024)S(1)}, f32[768]{0:T(1024)S(1)}) all-reduce(f32[3072]{0:T(1024)S(1)} %dynamic_update_slice.38, f32[3072]{0:T(1024)S(1)} %dynamic_update_slice.37, f32[768]{0:T(1024)S(1)} %dynamic_update_slice.40, ...), channel_id=32, replica_groups=mesh['fsdp'=16,'tp'=2] {'fsdp'}, use_global_device_ids=true, to_apply=%region_65.66.clone | all-reduce | flops 7680 | bytes 61440
  817.5 46.3 %reduce-scatter.55.cloned.1.call-done = f32[48,5]{1,0:T(8,128)} async-done(((f32[768,5]{1,0:T(8,128)}), f32[48,5]{1,0:T(8,128)}) %reduce-scatter.55.cloned.1.call-update) | async-done | bytes 976
  864.5 8.7 all-reduce.12
  873.8 8.6 reduce-scatter.41.cloned.1.call-done
  884.3 59.8 %reduce-scatter.45.cloned.1.call-done = f32[48,384]{1,0:T(8,128)} async-done(((f32[768,384]{1,0:T(8,128)}), f32[48,384]{1,0:T(8,128)}) %reduce-scatter.45.cloned.1.call-update) | async-done | bytes 73744 | tf_op jit(solution)/shard_map/reduce_scatter | solution.py:488
  944.1 60.6 %reduce-scatter.43.cloned.1.call-done = f32[48,384]{1,0:T(8,128)} async-done(((f32[768,384]{1,0:T(8,128)}), f32[48,384]{1,0:T(8,128)}) %reduce-scatter.43.cloned.1.call-update) | async-done | bytes 73744 | tf_op jit(solution)/shard_map/reduce_scatter | solution.py:488
  1006.3 186.1 %all-reduce.16.cloned.1.call-done = (f32[768,3,384]{2,1,0:T(4,128)}, f32[768,3,384]{2,1,0:T(4,128)}) async-done(((f32[768,3,384]{2,1,0:T(4,128)}, f32[768,3,384]{2,1,0:T(4,128)}), (f32[768,3,384]{2,1,0:T(4,128)}, f32[768,3,384]{2,1,0:T(4,128)})) %all-reduce.16.cloned.1.call-update) | async-done | bytes 7077904
  1195.3 77.0 %reduce-scatter.53.cloned.1.call-done = f32[48,1536]{1,0:T(8,128)} async-done(((f32[768,1536]{1,0:T(8,128)}), f32[48,1536]{1,0:T(8,128)}) %reduce-scatter.53.cloned.1.call-update) | async-done | bytes 294928 | tf_op jit(solution)/shard_map/reduce_scatter | solution.py:490
  1272.3 78.3 %reduce-scatter.51.cloned.1.call-done = f32[48,1536]{1,0:T(8,128)} async-done(((f32[768,1536]{1,0:T(8,128)}), f32[48,1536]{1,0:T(8,128)}) %reduce-scatter.51.cloned.1.call-update) | async-done | bytes 294928 | tf_op jit(solution)/shard_map/reduce_scatter | solution.py:490
  1352.5 76.9 %reduce-scatter.49.cloned.1.call-done = f32[48,1536]{1,0:T(8,128)} async-done(((f32[768,1536]{1,0:T(8,128)}), f32[48,1536]{1,0:T(8,128)}) %reduce-scatter.49.cloned.1.call-update) | async-done | bytes 294928 | tf_op jit(solution)/shard_map/reduce_scatter | solution.py:489
  1429.4 78.4 %reduce-scatter.47.cloned.1.call-done = f32[48,1536]{1,0:T(8,128)} async-done(((f32[768,1536]{1,0:T(8,128)}), f32[48,1536]{1,0:T(8,128)}) %reduce-scatter.47.cloned.1.call-update) | async-done | bytes 294928 | tf_op jit(solution)/shard_map/reduce_scatter | solution.py:489
  (410 shorter events, 131.6 us)
Async XLA Ops:
  7.2 325.2 %reduce-scatter.27.cloned.1.call-start = ((), (), s32[]{:S(2)}) async-start(), calls=%async_computation.18 | async-start | bytes 1179648 | tf_op jit(solution)/shard_map/reduce_scatter | solution.py:276
  147.1 111.0 %copy-start.9 = (f32[512,1,384]{0,2,1:T(8,128)}, f32[512,1,384]{0,2,1:T(8,128)S(1)}, u32[]{:S(2)}) copy-start(f32[512,1,384]{0,2,1:T(8,128)S(1)} %get-tuple-element.232) | copy-start | bytes 2359300
  147.1 112.3 %copy-start.32 = (f32[512,1,384]{0,2,1:T(8,128)}, f32[512,1,384]{0,2,1:T(8,128)S(1)}, u32[]{:S(2)}) copy-start(f32[512,1,384]{0,2,1:T(8,128)S(1)} %get-tuple-element.231) | copy-start | bytes 2359300
  232.4 25.7 %copy-start.17 = (bf16[1,5,768]{1,0,2:T(2,128)(2,1)}, bf16[1,5,768]{1,0,2:T(2,128)(2,1)S(1)}, u32[]{:S(2)}) copy-start(bf16[1,5,768]{1,0,2:T(2,128)(2,1)S(1)} %all-gather.5) | copy-start | bytes 23044
  262.8 12.1 copy-start.52
  265.5 104.3 %reduce-scatter.29.cloned.1.call-start = ((), (), s32[]{:S(2)}) async-start(), calls=%async_computation.19 | async-start | bytes 1179648 | tf_op jit(solution)/shard_map/reduce_scatter | solution.py:276
  266.0 8.9 copy-start.90
  300.6 7.0 copy-start.86
  324.9 5.0 slice-start.4
  324.9 5.0 slice-start.5
  332.4 15.9 %copy-start.38 = (bf16[1,768,4,384]{1,3,2,0:T(8,128)(2,1)S(1)}, bf16[1,768,4,384]{1,3,2,0:T(8,128)(2,1)}, u32[]{:S(2)}) copy-start(bf16[1,768,4,384]{1,3,2,0:T(8,128)(2,1)} %get-tuple-element.226) | copy-start | bytes 7077892
  333.7 36.1 %copy-start.68 = (f32[256]{0:T(256)}, f32[256]{0:T(256)S(1)}, u32[]{:S(2)}) copy-start(f32[256]{0:T(256)S(1)} %broadcast_multiply_fusion.12) | copy-start | bytes 3076
  335.0 34.8 %copy-start.70 = (f32[256]{0:T(256)}, f32[256]{0:T(256)S(1)}, u32[]{:S(2)}) copy-start(f32[256]{0:T(256)S(1)} %add_rsqrt_fusion.3) | copy-start | bytes 3076
  348.3 4.2 copy-start.36
  352.5 17.3 %copy-start.5 = (bf16[256,768]{1,0:T(8,128)(2,1)S(1)}, bf16[256,768]{1,0:T(8,128)(2,1)}, u32[]{:S(2)}) copy-start(bf16[256,768]{1,0:T(8,128)(2,1)} %reduce-scatter.27.cloned.1.call-done) | copy-start | bytes 1179652
  354.8 80.5 %reduce-scatter.31.cloned.1.call-start = ((), (), s32[]{:S(2)}) async-start(), calls=%async_computation.20 | async-start | bytes 1179648 | tf_op jit(solution)/shard_map/reduce_scatter | solution.py:276
  369.8 14.5 copy-start.4
  389.5 4.8 copy-start.18
  391.5 26.3 %copy-start.85 = (bf16[3072]{0:T(1024)(128)(2,1)S(1)}, bf16[3072]{0:T(1024)(128)(2,1)}, u32[]{:S(2)}) copy-start(bf16[3072]{0:T(1024)(128)(2,1)} %get-tuple-element.204) | copy-start | bytes 18436
  394.2 100.0 %reduce-scatter.33.cloned.1.call-start = ((), (), s32[]{:S(2)}) async-start(), calls=%async_computation.21 | async-start | bytes 1179648 | tf_op jit(solution)/shard_map/reduce_scatter | solution.py:276
  435.3 14.0 copy-start.42
  449.3 4.2 copy-start.40
  455.8 79.5 %reduce-scatter.35.cloned.1.call-start = ((), (), s32[]{:S(2)}) async-start(), calls=%async_computation.22 | async-start | bytes 1179648 | tf_op jit(solution)/shard_map/reduce_scatter | solution.py:289
  494.3 4.3 copy-start.55
  495.7 15.2 copy-start.41
  495.7 15.2 copy-start.93
  510.9 4.0 copy-start.43
  517.2 72.3 %reduce-scatter.37.cloned.1.call-start = ((), (), s32[]{:S(2)}) async-start(), calls=%async_computation.23 | async-start | bytes 1179648 | tf_op jit(solution)/shard_map/reduce_scatter | solution.py:289
  540.0 18.0 %slice-start.2 = ((s8[6291456]{0:T(1024)(128)(4,1)}), s8[4194304]{0:T(1024)(128)(4,1)S(1)}, s32[]{:S(2)}) async-start(s8[6291456]{0:T(1024)(128)(4,1)} %bitcast.228), calls=%async_computation.39 | async-start | bytes 8388608
  551.8 6.2 copy-start.28
  553.7 4.4 slice-start.3
  553.7 4.4 copy-start.35
  558.1 10.7 copy-start.58
  562.3 4.8 copy-start.12
  568.8 20.7 %copy-start.15 = (f32[256,768]{1,0:T(8,128)S(1)}, f32[256,768]{1,0:T(8,128)}, u32[]{:S(2)}) copy-start(f32[256,768]{1,0:T(8,128)} %get-tuple-element.210) | copy-start | bytes 2359300
  572.0 64.3 %reduce-scatter.39.cloned.1.call-start = ((), (), s32[]{:S(2)}) async-start(), calls=%async_computation.24 | async-start | bytes 1179648 | tf_op jit(solution)/shard_map/reduce_scatter | solution.py:289
  589.5 15.9 %copy-start.37 = (bf16[1,768,4,384]{1,3,2,0:T(8,128)(2,1)S(1)}, bf16[1,768,4,384]{1,3,2,0:T(8,128)(2,1)}, u32[]{:S(2)}) copy-start(bf16[1,768,4,384]{1,3,2,0:T(8,128)(2,1)} %get-tuple-element.224) | copy-start | bytes 7077892
  589.5 15.9 %copy-start.92 = (f32[512,1536]{1,0:T(8,128)S(1)}, f32[512,1536]{1,0:T(8,128)}, u32[]{:S(2)}) copy-start(f32[512,1536]{1,0:T(8,128)} %get-tuple-element.249) | copy-start | bytes 9437188
  605.5 4.0 copy-start.39
  611.7 24.6 %copy-start.69 = (f32[256]{0:T(256)S(1)}, f32[256]{0:T(256)}, u32[]{:S(2)}) copy-start(f32[256]{0:T(256)} %copy-done.68) | copy-start | bytes 3076
  611.8 43.0 %slice-start = ((s8[6291456]{0:T(1024)(128)(4,1)}), s8[2097152]{0:T(1024)(128)(4,1)S(1)}, s32[]{:S(2)}) async-start(s8[6291456]{0:T(1024)(128)(4,1)} %bitcast.226), calls=%async_computation.37 | async-start | bytes 4194304
  611.8 142.1 %reduce-scatter.61.cloned.1.call-start = ((), (), s32[]{:S(2)}) async-start(), calls=%async_computation.35 | async-start | bytes 417792
  624.0 131.0 %reduce-scatter.57.cloned.1.call-start = ((), (), s32[]{:S(2)}) async-start(), calls=%async_computation.33 | async-start | bytes 417792
  636.1 180.6 %reduce-scatter.59.cloned.1.call-start = ((), (), s32[]{:S(2)}) async-start(), calls=%async_computation.34 | async-start | bytes 417792
  636.4 18.4 %slice-start.1 = ((s8[6291456]{0:T(1024)(128)(4,1)}), s8[4194304]{0:T(1024)(128)(4,1)S(1)}, s32[]{:S(2)}) async-start(s8[6291456]{0:T(1024)(128)(4,1)} %bitcast.226), calls=%async_computation.38 | async-start | bytes 8388608
  639.0 15.8 %copy-start.65 = (f32[6,512]{1,0:T(8,128)S(1)}, f32[6,512]{1,0:T(8,128)}, u32[]{:S(2)}) copy-start(f32[6,512]{1,0:T(8,128)} %log_add_fusion) | copy-start | bytes 36868
  652.8 4.1 copy-start.30
  663.0 3.7 copy-start.7
  664.1 199.7 %reduce-scatter.55.cloned.1.call-start = ((), (), s32[]{:S(2)}) async-start(), calls=%async_computation.32 | async-start | bytes 417792
  665.5 216.9 %reduce-scatter.41.cloned.1.call-start = ((), (), s32[]{:S(2)}) async-start(), calls=%async_computation.25 | async-start | bytes 1179648 | tf_op jit(solution)/shard_map/reduce_scatter | solution.py:289
  668.9 4.8 copy-start.59
  668.9 275.2 %reduce-scatter.45.cloned.1.call-start = ((), (), s32[]{:S(2)}) async-start(), calls=%async_computation.27 | async-start | bytes 1253376 | tf_op jit(solution)/shard_map/reduce_scatter | solution.py:488
  671.7 333.0 %reduce-scatter.43.cloned.1.call-start = ((), (), s32[]{:S(2)}) async-start(), calls=%async_computation.26 | async-start | bytes 1253376 | tf_op jit(solution)/shard_map/reduce_scatter | solution.py:488
  673.4 519.0 %all-reduce.16.cloned.1.call-start = ((), (), s32[]{:S(2)}) async-start(), calls=%async_computation.36 | async-start | bytes 18874368
  676.1 4.6 copy-start.57
  676.1 4.6 copy-start.61
  689.9 582.3 %reduce-scatter.53.cloned.1.call-start = ((), (), s32[]{:S(2)}) async-start(), calls=%async_computation.31 | async-start | bytes 5013504 | tf_op jit(solution)/shard_map/reduce_scatter | solution.py:490
  695.1 655.4 %reduce-scatter.51.cloned.1.call-start = ((), (), s32[]{:S(2)}) async-start(), calls=%async_computation.30 | async-start | bytes 5013504 | tf_op jit(solution)/shard_map/reduce_scatter | solution.py:490
  700.5 729.0 %reduce-scatter.49.cloned.1.call-start = ((), (), s32[]{:S(2)}) async-start(), calls=%async_computation.29 | async-start | bytes 5013504 | tf_op jit(solution)/shard_map/reduce_scatter | solution.py:489
  705.7 802.2 %reduce-scatter.47.cloned.1.call-start = ((), (), s32[]{:S(2)}) async-start(), calls=%async_computation.28 | async-start | bytes 5013504 | tf_op jit(solution)/shard_map/reduce_scatter | solution.py:489
  711.0 42.3 %copy-start.82 = (f32[1536]{0:T(1024)S(1)}, f32[1536]{0:T(1024)}, u32[]{:S(2)}) copy-start(f32[1536]{0:T(1024)} %get-tuple-element.258) | copy-start | bytes 18436
  711.0 42.7 %copy-start.81 = (f32[384]{0:T(512)S(1)}, f32[384]{0:T(512)}, u32[]{:S(2)}) copy-start(f32[384]{0:T(512)} %get-tuple-element.236) | copy-start | bytes 4612
  711.0 43.7 %copy-start.83 = (f32[1536]{0:T(1024)S(1)}, f32[1536]{0:T(1024)}, u32[]{:S(2)}) copy-start(f32[1536]{0:T(1024)} %get-tuple-element.260) | copy-start | bytes 18436
  711.0 171.4 %copy-start.14 = (f32[256,768]{1,0:T(8,128)S(1)}, f32[256,768]{1,0:T(8,128)}, u32[]{:S(2)}) copy-start(f32[256,768]{1,0:T(8,128)} %copy-done.13) | copy-start | bytes 2359300
  (55 other events, 113.9 us)
Sparse Core Ops, SparseCore 0:
  265.6 13.7 reduce-scatter.26
  354.9 14.8 reduce-scatter.28
  394.3 17.4 reduce-scatter.30
  455.9 14.2 reduce-scatter.32
  517.4 17.8 reduce-scatter.34
  572.1 17.3 reduce-scatter.36
  611.9 17.4 reduce-scatter.38
  633.3 55.5 reduce-scatter.60
  692.4 54.6 reduce-scatter.56
  750.8 54.6 reduce-scatter.58
  809.1 54.6 reduce-scatter.54
  865.9 16.4 reduce-scatter.40
  886.0 58.0 reduce-scatter.44
  947.6 57.0 reduce-scatter.42
  1008.3 184.1 all-reduce.15
  1196.6 75.5 reduce-scatter.52
  1276.0 74.5 reduce-scatter.50
  1354.8 74.5 reduce-scatter.48
  1433.3 74.5 reduce-scatter.46
